TPU v7x, 256 devices: a whole 4x4x8 slice. The times are simulated.
256 devices in a mesh: obs: 64 (over x, z, core), tile: 4 (over y).
Axes of the slice: x: 4, y: 4, z: 8, core: 2. Of those that a mesh axis runs over, the one named last changes fastest.
Arguments:
- jacobian: bfloat16 [16384, 65536], P(('obs', 'tile')), may hold values from -0.1875 to 0.1875
- obs_weight: float32 [16384], P(('obs', 'tile')), may hold values from 0.1 to 10
- block_order: int32 [512], replicated, may hold values from 0 to 511, each once
- tile_pairs: int32 [64, 64, 2], P('obs'), may hold values from 0 to 7, as said below
- tile_count: int32 [64], P('obs'), may hold values from 1 to 64, as said below
Outputs:
- hessian: float32 [4096, 128, 128], P(('obs', 'tile'))
Inputs may be any that keep to these rules, and one draw needn't show every extreme that they name: `tile_pairs`: slot numbers within an owner's own 8 slots; the first tile_count[j] pairs of owner j are distinct. `tile_count`: some owner has 64 live tiles.
All inputs are finite; a program needn't handle non-finite values.
Results may differ from a plain program's by a relative error of at most 0.0015.
Values may be sent and summed in bfloat16 or wider, within the bound.
No kernel may reach another device: no remote copies, remote signals or barrier semaphores. Data moves between devices by JAX's collectives and lax.ppermute only.
A program may use at most 256 MiB of HBM per device.

v0:
```python
import jax
import jax.numpy as jnp
from jax import lax
from jax.sharding import PartitionSpec as P

BLOCK = 128


def body(jacobian, obs_weight, block_order, tile_pairs, tile_count):
    row_count = jacobian.shape[0]
    owners = lax.axis_size("obs")
    total_blocks = block_order.shape[0]
    own_blocks = total_blocks // owners
    own_width = own_blocks * BLOCK
    blocks = jacobian.reshape(row_count, total_blocks, BLOCK)
    ordered = jnp.take(blocks, block_order, axis=1)
    root_weight = jnp.sqrt(obs_weight)[:, None, None]
    scaled = (ordered.astype(jnp.float32) * root_weight).astype(jnp.bfloat16)
    outgoing = scaled.reshape(row_count, owners, own_width)
    arrived = lax.all_to_all(outgoing, "obs", split_axis=1, concat_axis=0, tiled=True)
    columns = arrived.reshape(row_count * owners, own_width)
    pair_list = tile_pairs[0]
    live_count = tile_count[0]
    slot_total = pair_list.shape[0]
    slot_ids = jnp.arange(slot_total, dtype=jnp.int32)
    is_live = slot_ids < live_count
    per_group = min(own_blocks, 8)

    def gram_group(group_index, tiles):
        first_slot = group_index * per_group
        gram_part = lax.dot_general(
            columns, columns, (((0,), (0,)), ((), ())), preferred_element_type=jnp.float32
        )
        gram_tiles = gram_part.reshape(per_group, BLOCK, own_blocks, BLOCK).transpose(0, 2, 1, 3)
        gram_tiles = gram_tiles.reshape(per_group * own_blocks, BLOCK, BLOCK)
        relative = pair_list[:, 0] - first_slot
        inside = (relative >= 0) & (relative < per_group) & is_live
        lookup = jnp.clip(relative, 0, per_group - 1) * own_blocks + pair_list[:, 1]
        picked = jnp.take(gram_tiles, lookup, axis=0)
        return jnp.where(inside[:, None, None], picked, tiles)

    all_tiles = lax.fori_loop(
        0, own_blocks // per_group, gram_group, jnp.zeros((slot_total, BLOCK, BLOCK), jnp.float32)
    )
    hessian = lax.psum_scatter(all_tiles, "tile", scatter_dimension=0, tiled=True)
    return hessian


def solution(mesh):
    return jax.shard_map(
        body,
        mesh=mesh,
        in_specs=(
            P(("obs", "tile"), None),
            P(("obs", "tile")),
            P(),
            P("obs", None, None),
            P("obs"),
        ),
        out_specs=P(("obs", "tile"), None, None),
        check_vma=False,
    )
```

profile of v0, /device:TPU:1, one launch (start us, length us, event | category | flops | bytes accessed | tf_op | source)
XLA Modules:
  0.0 376.2 jit_solution(16123092588798176954)
XLA Ops:
  6.5 0.7 compare_select_fusion
  7.2 0.7 compare_and_fusion
  7.9 9.0 %copy_bitcast_fusion = bf16[64,512,128]{2,0,1:T(8,128)(2,1)} fusion(bf16[64,65536]{1,0:T(8,128)(2,1)} %param.5), kind=kLoop, calls=%fused_computation.3 | loop fusion | bytes 16777216 | tf_op jit(solution)/shard_map/reshape | solution.py:15
  16.9 23.0 %gather_fusion = bf16[512,64,128]{2,1,0:T(8,128)(2,1)} fusion(bf16[64,512,128]{2,0,1:T(8,128)(2,1)} %copy_bitcast_fusion, s32[1024]{0:T(1024)S(1)} %pad_clamp_fusion.1), kind=kCustom, calls=%fused_computation | custom fusion | bytes 16779264 | tf_op jit(solution)/shard_map/jit(_take)/gather | solution.py:16
  40.0 12.0 %copy.13 = bf16[64,512,128]{2,1,0:T(8,128)(2,1)} copy(bf16[64,512,128]{2,0,1:T(8,128)(2,1)} %bitcast.35) | data formatting | bytes 16777216 | tf_op jit(solution)/shard_map/jit(_take)/gather | solution.py:16
  52.0 0.0 copy-start.1
  52.0 13.3 %gather.12 = bf16[64,64,1024]{2,1,0:T(8,128)(2,1)} reshape(bf16[64,512,128]{2,1,0:T(8,128)(2,1)} %copy.13) | data formatting | bytes 16777216 | tf_op jit(solution)/shard_map/jit(_take)/gather | solution.py:16
  65.3 0.1 broadcast_in_dim.50
  65.4 0.1 broadcast_in_dim.51
  65.6 0.0 copy-done.1
  65.6 10.0 %multiply_convert_fusion = bf16[64,64,1024]{2,1,0:T(8,128)(2,1)} fusion(f32[64]{0:T(128)S(1)} %sqrt.3, bf16[64,64,1024]{2,1,0:T(8,128)(2,1)} %gather.12, pred[64,1024]{1,0:T(8,128)(4,1)S(1)} %bitcast.39), kind=kLoop, calls=%fused_computation.2 | loop fusion | flops 16777216 | bytes 16843008 | tf_op jit(solution)/shard_map/convert_element_type | solution.py:18
  75.6 11.3 %copy.14 = bf16[64,64,1024]{2,0,1:T(8,128)(2,1)} copy(bf16[64,64,1024]{2,1,0:T(8,128)(2,1)} %multiply_convert_fusion) | data formatting | bytes 16777216 | tf_op jit(solution)/shard_map/convert_element_type | solution.py:18
  86.9 0.0 copy-start
  86.9 13.3 %all-to-all-start = ((bf16[64,64,1024]{2,0,1:T(8,128)(2,1)}), bf16[64,64,1024]{2,0,1:T(8,128)(2,1)}, u32[]{:S(2)}, u32[]{:S(2)}) async-start(bf16[64,64,1024]{2,0,1:T(8,128)(2,1)} %copy.14), calls=%async_computation | async-start | bytes 16777216 | tf_op jit(solution)/shard_map/all_to_all | solution.py:20
  100.2 0.0 reduce-scatter.2.cloned.1.call-start
  100.9 0.0 copy-done
  100.9 185.0 %all-to-all-done = bf16[64,64,1024]{2,0,1:T(8,128)(2,1)} async-done(((bf16[64,64,1024]{2,0,1:T(8,128)(2,1)}), bf16[64,64,1024]{2,0,1:T(8,128)(2,1)}, u32[]{:S(2)}, u32[]{:S(2)}) %all-to-all-start) | async-done | bytes 8388640 | tf_op jit(solution)/shard_map/all_to_all | solution.py:20
  286.0 11.6 %copy.15 = bf16[1024,4096]{1,0:T(8,128)(2,1)} copy(bf16[1024,4096]{0,1:T(8,128)(2,1)} %bitcast.8) | data formatting | bytes 16777216 | tf_op jit(solution)/shard_map/while/body/eval_jaxpr/dot_general | solution.py:31
  297.5 15.9 %fusion = f32[8,128,8,128]{3,1,2,0:T(8,128)} fusion(bf16[8,128,4096,1]{2,1,3,0:T(8,128)(2,1)} %bitcast.36, bf16[8,128,4096,1]{2,1,0,3:T(8,128)(2,1)} %bitcast.37), kind=kOutput, calls=%fused_computation.13 | convolution fusion | flops 8589934592 | bytes 20971520 | tf_op jit(solution)/shard_map/while/body/eval_jaxpr/dot_general | solution.py:31
  313.4 5.0 %gather_fusion.1 = f32[64,128,128]{2,1,0:T(8,128)} fusion(f32[64,128,128]{2,1,0:T(8,128)} %bitcast.38, s32[1024]{0:T(1024)S(1)} %pad_clamp_fusion), kind=kCustom, calls=%fused_computation.1 | custom fusion | bytes 8388864 | tf_op jit(solution)/shard_map/while/body/eval_jaxpr/jit(_take)/gather | solution.py:39
  318.4 4.7 %select_select_fusion = f32[64,128,128]{2,1,0:T(8,128)} fusion(f32[64,128,128]{2,1,0:T(8,128)} %gather_fusion.1, pred[64]{0:T(512)(128)(4,1)S(1)} %get-tuple-element.15, pred[64]{0:T(512)(128)(4,1)S(1)} %bitcast_and_fusion), kind=kLoop, calls=%fused_computation.4 | loop fusion | flops 2097152 | bytes 8388736 | tf_op jit(solution)/shard_map/while/body/eval_jaxpr/jit(_where)/select_n | solution.py:40
  323.0 0.0 reduce-scatter.2.cloned.1.call-update
  323.0 46.3 %reduce-scatter.2.cloned.1.call-done = f32[16,128,128]{2,1,0:T(8,128)} async-done(((f32[64,128,128]{2,1,0:T(8,128)}), f32[16,128,128]{2,1,0:T(8,128)}) %reduce-scatter.2.cloned.1.call-update) | async-done | bytes 1048592 | tf_op jit(solution)/shard_map/reduce_scatter | solution.py:45
  (6 shorter events, 0.1 us)
Async XLA Ops:
  52.0 13.6 %copy-start.1 = (f32[64]{0:T(128)S(1)}, f32[64]{0:T(128)}, u32[]{:S(2)}) copy-start(f32[64]{0:T(128)} %param.6) | copy-start | bytes 772
  86.9 14.0 %copy-start = (s32[1,64,2]{1,2,0:T(2,128)S(1)}, s32[1,64,2]{1,2,0:T(2,128)}, u32[]{:S(2)}) copy-start(s32[1,64,2]{1,2,0:T(2,128)} %param.8) | copy-start | bytes 1540
  86.9 199.1 %all-to-all-start = ((bf16[64,64,1024]{2,0,1:T(8,128)(2,1)}), bf16[64,64,1024]{2,0,1:T(8,128)(2,1)}, u32[]{:S(2)}, u32[]{:S(2)}) async-start(bf16[64,64,1024]{2,0,1:T(8,128)(2,1)} %copy.14), calls=%async_computation | async-start | bytes 16777216 | tf_op jit(solution)/shard_map/all_to_all | solution.py:20
  100.2 269.2 %reduce-scatter.2.cloned.1.call-start = ((), (), s32[]{:S(2)}) async-start(), calls=%async_computation.2 | async-start | bytes 5242880 | tf_op jit(solution)/shard_map/reduce_scatter | solution.py:45
Sparse Core Ops, SparseCore 0:
  323.2 46.1 reduce-scatter.1
where the time goes:
time: 377 us; the launch traced here: 376 us
  waiting for transfers between devices  231 us (61%)
  local copies, waits for them, and re-layouts  85.5 us (23%)
  other arithmetic  16 us (4%)
  matrix products  15.9 us (4%)
  between operations  14.1 us (4%)
  starting transfers between devices  13.3 us (4%)
    all_to_all x1, waiting for transfers between devices, body(): lax.all_to_all(outgoing, 'obs', split_axis=1, concat_axis=0, tiled=True)  185 us
    gather x3, local copies, waits for them, and re-layouts, body(): ordered = jnp.take(blocks, block_order, axis=1)  48.4 us
    reduce_scatter x1, waiting for transfers between devices, body(): lax.psum_scatter(all_tiles, 'tile', scatter_dimension=0, tiled=True)  46.3 us
    dot_general x1, matrix products, gram_group(): lax.dot_general(columns, columns, (((0,), (0,)), ((), ())), preferred_ele...  15.9 us
    all_to_all x1, starting transfers between devices, body(): lax.all_to_all(outgoing, 'obs', split_axis=1, concat_axis=0, tiled=True)  13.3 us
    dot_general x1, local copies, waits for them, and re-layouts, gram_group(): lax.dot_general(columns, columns, (((0,), (0,)), ((), ())), preferred_ele...  11.6 us
    convert_element_type x1, local copies, waits for them, and re-layouts, body(): scaled = (ordered.astype(jnp.float32) * root_weight).astype(jnp.bfloat16)  11.3 us
    convert_element_type x1, other arithmetic, body(): scaled = (ordered.astype(jnp.float32) * root_weight).astype(jnp.bfloat16)  9.97 us
  transfers between devices with their start and end apart: 2, of which 2 were waited for; matrix products, arithmetic and copies ran while one was open for 0% of the time, Pallas kernels for 0%

commit v1 on v0

--- a/solution.py
+++ b/solution.py
@@ -17,7 +17,9 @@
     root_weight = jnp.sqrt(obs_weight)[:, None, None]
     scaled = (ordered.astype(jnp.float32) * root_weight).astype(jnp.bfloat16)
     outgoing = scaled.reshape(row_count, owners, own_width)
-    arrived = lax.all_to_all(outgoing, "obs", split_axis=1, concat_axis=0, tiled=True)
+    pieces = jnp.split(outgoing, lax.axis_size("obs"), axis=1)
+    received = lax.all_to_all(jnp.stack(pieces), "obs", 0, 0)
+    arrived = jnp.concatenate(received, axis=0)
     columns = arrived.reshape(row_count * owners, own_width)
     pair_list = tile_pairs[0]
     live_count = tile_count[0]

time: 377 us -> 439 us (1.16)
  local copies, waits for them, and re-layouts: 85.5 us -> 147 us
    unnamed x5 -> x70, local copies, waits for them, and re-layouts: 0.04 us -> 43.7 us
    split x0 -> x4, local copies, waits for them, and re-layouts: none -> 28.3 us  [body(): pieces = jnp.split(outgoing, lax.axis_size('obs'), axis=1)]
    convert_element_type x1 -> x0, local copies, waits for them, and re-layouts: 11.3 us -> none  [body(): scaled = (ordered.astype(jnp.float32) * root_weight).astype(jnp.bfloat16)]
where the time goes in v1:
time: 439 us; the launch traced here: 438 us
  waiting for transfers between devices  231 us (53%)
  local copies, waits for them, and re-layouts  147 us (33%)
  other arithmetic  16.7 us (4%)
  matrix products  15.9 us (4%)
  between operations  14.2 us (3%)
  starting transfers between devices  13.3 us (3%)
    all_to_all x1, waiting for transfers between devices, body(): received = lax.all_to_all(jnp.stack(pieces), 'obs', 0, 0)  185 us
    gather x3, local copies, waits for them, and re-layouts, body(): ordered = jnp.take(blocks, block_order, axis=1)  48.4 us
    reduce_scatter x1, waiting for transfers between devices, body(): lax.psum_scatter(all_tiles, 'tile', scatter_dimension=0, tiled=True)  46.3 us
    unnamed x70, local copies, waits for them, and re-layouts  43.7 us
    split x4, local copies, waits for them, and re-layouts, body(): pieces = jnp.split(outgoing, lax.axis_size('obs'), axis=1)  28.3 us
    dot_general x1, matrix products, gram_group(): lax.dot_general(columns, columns, (((0,), (0,)), ((), ())), preferred_ele...  15.9 us
    all_to_all x1, starting transfers between devices, body(): received = lax.all_to_all(jnp.stack(pieces), 'obs', 0, 0)  13.3 us
    dot_general x1, local copies, waits for them, and re-layouts, gram_group(): lax.dot_general(columns, columns, (((0,), (0,)), ((), ())), preferred_ele...  11.3 us
  transfers between devices with their start and end apart: 2, of which 2 were waited for; matrix products, arithmetic and copies ran while one was open for 0% of the time, Pallas kernels for 0%

profile of v1, /device:TPU:1, one launch (start us, length us, event | category | flops | bytes accessed | tf_op | source)
XLA Modules:
  0.0 438.3 jit_solution(5040270233363908134)
XLA Ops:
  7.9 0.8 and_bitcast_fusion
  8.7 9.0 %copy_bitcast_fusion = bf16[64,512,128]{2,0,1:T(8,128)(2,1)} fusion(bf16[64,65536]{1,0:T(8,128)(2,1)} %param.5), kind=kLoop, calls=%fused_computation.3 | loop fusion | bytes 16777216 | tf_op jit(solution)/shard_map/reshape | solution.py:15
  17.7 23.0 %gather_fusion = bf16[512,64,128]{2,1,0:T(8,128)(2,1)} fusion(bf16[64,512,128]{2,0,1:T(8,128)(2,1)} %copy_bitcast_fusion, s32[1024]{0:T(1024)S(1)} %get-tuple-element.90), kind=kCustom, calls=%fused_computation | custom fusion | bytes 16779264 | tf_op jit(solution)/shard_map/jit(_take)/gather | solution.py:16
  40.8 12.0 %copy.1551 = bf16[64,512,128]{2,1,0:T(8,128)(2,1)} copy(bf16[64,512,128]{2,0,1:T(8,128)(2,1)} %bitcast.159) | data formatting | bytes 16777216 | tf_op jit(solution)/shard_map/jit(_take)/gather | solution.py:16
  52.8 13.4 %gather.12 = bf16[64,64,1024]{2,1,0:T(8,128)(2,1)} reshape(bf16[64,512,128]{2,1,0:T(8,128)(2,1)} %copy.1551) | data formatting | bytes 16777216 | tf_op jit(solution)/shard_map/jit(_take)/gather | solution.py:16
  66.4 10.0 %multiply_convert_fusion = bf16[64,64,1024]{2,1,0:T(8,128)(2,1)} fusion(f32[64]{0:T(128)S(1)} %sqrt.3, bf16[64,64,1024]{2,1,0:T(8,128)(2,1)} %gather.12, pred[64,1024]{1,0:T(8,128)(4,1)S(1)} %bitcast.163), kind=kLoop, calls=%fused_computation.2 | loop fusion | flops 16777216 | bytes 16843008 | tf_op jit(solution)/shard_map/convert_element_type | solution.py:18
  76.4 5.6 %fusion.3 = (bf16[64,1,1024]{2,1,0:T(2,128)(2,1)S(1)}, bf16[64,1,1024]{2,1,0:T(2,128)(2,1)S(1)}, bf16[64,1,1024]{2,1,0:T(2,128)(2,1)S(1)}, bf16[64,1,1024]{2,1,0...) fusion(bf16[64,64,1024]{2,1,0:T(8,128)(2,1)} %multiply_convert_, ...), kind=kLoop, calls=%fused_computation.80 | loop fusion | bytes 1835008 | tf_op jit(solution)/shard_map/split | solution.py:20
  82.0 11.9 %fusion.2 = (bf16[64,1,1024]{2,1,0:T(2,128)(2,1)S(1)}, bf16[64,1,1024]{2,1,0:T(2,128)(2,1)S(1)}, bf16[64,1,1024]{2,1,0:T(2,128)(2,1)S(1)}, bf16[64,1,1024]{2,1,0...) fusion(bf16[64,64,1024]{2,1,0:T(8,128)(2,1)} %multiply_convert_, ...), kind=kLoop, calls=%fused_computation.79 | loop fusion | bytes 4980736 | tf_op jit(solution)/shard_map/split | solution.py:20
  93.9 5.1 %fusion.1 = (bf16[64,1,1024]{2,1,0:T(2,128)(2,1)S(1)}, bf16[64,1,1024]{2,1,0:T(2,128)(2,1)S(1)}, bf16[64,1,1024]{2,1,0:T(2,128)(2,1)S(1)}, bf16[64,1,1024]{2,1,0...) fusion(bf16[64,64,1024]{2,1,0:T(8,128)(2,1)S(1)} %copy-done), kind=kLoop, calls=%fused_computation.78 | loop fusion | bytes 4980736 | tf_op jit(solution)/shard_map/split | solution.py:20
  99.0 5.7 %fusion = (bf16[64,1,1024]{2,1,0:T(2,128)(2,1)S(1)}, bf16[64,1,1024]{2,1,0:T(2,128)(2,1)S(1)}, bf16[64,1,1024]{2,1,0:T(2,128)(2,1)S(1)}, bf16[64,1,1024]{2,1,0:T...) fusion(bf16[64,64,1024]{2,1,0:T(8,128)(2,1)S(1)} %copy-done), kind=kLoop, calls=%fused_computation.77 | loop fusion | bytes 4980736 | tf_op jit(solution)/shard_map/split | solution.py:20
  108.2 0.7 constant_dynamic-update-slice_fusion.58
  113.8 0.7 constant_dynamic-update-slice_fusion.50
  117.9 0.7 constant_dynamic-update-slice_fusion.44
  122.1 0.7 constant_dynamic-update-slice_fusion.38
  124.2 0.7 constant_dynamic-update-slice_fusion.35
  126.9 0.7 constant_dynamic-update-slice_fusion.31
  128.3 0.7 constant_dynamic-update-slice_fusion.29
  132.5 0.7 constant_dynamic-update-slice_fusion.23
  135.2 0.7 constant_dynamic-update-slice_fusion.19
  137.3 0.7 constant_dynamic-update-slice_fusion.16
  138.0 0.7 constant_dynamic-update-slice_fusion.15
  142.2 0.7 constant_dynamic-update-slice_fusion.9
  145.6 0.7 constant_dynamic-update-slice_fusion.4
  147.7 0.7 constant_dynamic-update-slice_fusion.1
  148.4 0.7 constant_dynamic-update-slice_fusion
  149.1 13.3 %all-to-all-start = ((bf16[64,64,1,1024]{3,1,2,0:T(8,128)(2,1)}), bf16[64,64,1,1024]{3,1,2,0:T(8,128)(2,1)}, u32[]{:S(2)}, u32[]{:S(2)}) async-start(bf16[64,64,1,1024]{3,1,2,0:T(8,128)(2,1)} %constant_dynamic-update-slice_fusion), calls=%async_computation | async-start | bytes 16777216 | tf_op jit(solution)/shard_map/all_to_all | solution.py:21
  163.2 185.0 %all-to-all-done = bf16[64,64,1,1024]{3,1,2,0:T(8,128)(2,1)} async-done(((bf16[64,64,1,1024]{3,1,2,0:T(8,128)(2,1)}), bf16[64,64,1,1024]{3,1,2,0:T(8,128)(2,1)}, u32[]{:S(2)}, u32[]{:S(2)}) %all-to-all-start) | async-done | bytes 8388640 | tf_op jit(solution)/shard_map/all_to_all | solution.py:21
  348.2 11.3 %copy.1552 = bf16[1024,4096]{1,0:T(8,128)(2,1)} copy(bf16[1024,4096]{0,1:T(8,128)(2,1)} %bitcast.6) | data formatting | bytes 16777216 | tf_op jit(solution)/shard_map/while/body/eval_jaxpr/dot_general | solution.py:33
  359.5 15.9 %fusion.4 = f32[8,128,8,128]{3,1,2,0:T(8,128)} fusion(bf16[8,128,4096,1]{2,1,3,0:T(8,128)(2,1)} %bitcast.160, bf16[8,128,4096,1]{2,1,0,3:T(8,128)(2,1)} %bitcast.161), kind=kOutput, calls=%fused_computation.81 | convolution fusion | flops 8589934592 | bytes 20971520 | tf_op jit(solution)/shard_map/while/body/eval_jaxpr/dot_general | solution.py:33
  375.5 5.0 %gather_fusion.1 = f32[64,128,128]{2,1,0:T(8,128)} fusion(f32[64,128,128]{2,1,0:T(8,128)} %bitcast.162, s32[1024]{0:T(1024)S(1)} %get-tuple-element.89), kind=kCustom, calls=%fused_computation.1 | custom fusion | bytes 8388864 | tf_op jit(solution)/shard_map/while/body/eval_jaxpr/jit(_take)/gather | solution.py:41
  380.4 4.6 %select_select_fusion = f32[64,128,128]{2,1,0:T(8,128)} fusion(f32[64,128,128]{2,1,0:T(8,128)} %gather_fusion.1, pred[64]{0:T(512)(128)(4,1)S(1)} %get-tuple-element.15, pred[64]{0:T(512)(128)(4,1)S(1)} %bitcast_and_fusion), kind=kLoop, calls=%fused_computation.4 | loop fusion | flops 2097152 | bytes 8388736 | tf_op jit(solution)/shard_map/while/body/eval_jaxpr/jit(_where)/select_n | solution.py:42
  385.1 46.3 %reduce-scatter.2.cloned.1.call-done = f32[16,128,128]{2,1,0:T(8,128)} async-done(((f32[64,128,128]{2,1,0:T(8,128)}), f32[16,128,128]{2,1,0:T(8,128)}) %reduce-scatter.2.cloned.1.call-update) | async-done | bytes 1048592 | tf_op jit(solution)/shard_map/reduce_scatter | solution.py:47
  (65 shorter events, 35.6 us)
Async XLA Ops:
  52.8 13.7 %copy-start.2 = (f32[64]{0:T(128)S(1)}, f32[64]{0:T(128)}, u32[]{:S(2)}) copy-start(f32[64]{0:T(128)} %param.6) | copy-start | bytes 772
  76.4 17.5 %copy-start = (bf16[64,64,1024]{2,1,0:T(8,128)(2,1)S(1)}, bf16[64,64,1024]{2,1,0:T(8,128)(2,1)}, u32[]{:S(2)}) copy-start(bf16[64,64,1024]{2,1,0:T(8,128)(2,1)} %multiply_convert_fusion) | copy-start | bytes 25165828
  149.1 14.0 %copy-start.1 = (s32[1,64,2]{1,2,0:T(2,128)S(1)}, s32[1,64,2]{1,2,0:T(2,128)}, u32[]{:S(2)}) copy-start(s32[1,64,2]{1,2,0:T(2,128)} %param.8) | copy-start | bytes 1540
  149.1 199.1 %all-to-all-start = ((bf16[64,64,1,1024]{3,1,2,0:T(8,128)(2,1)}), bf16[64,64,1,1024]{3,1,2,0:T(8,128)(2,1)}, u32[]{:S(2)}, u32[]{:S(2)}) async-start(bf16[64,64,1,1024]{3,1,2,0:T(8,128)(2,1)} %constant_dynamic-update-slice_fusion), calls=%async_computation | async-start | bytes 16777216 | tf_op jit(solution)/shard_map/all_to_all | solution.py:21
  162.4 269.0 %reduce-scatter.2.cloned.1.call-start = ((), (), s32[]{:S(2)}) async-start(), calls=%async_computation.2 | async-start | bytes 5242880 | tf_op jit(solution)/shard_map/reduce_scatter | solution.py:47
Sparse Core Ops, SparseCore 0:
  385.2 46.1 reduce-scatter.1
